TPU v7x, 32 devices: a whole 2x2x4 slice. The times are simulated.
32 devices in a mesh: groups: 2 (over x), mem: 16 (over z, y, core).
Axes of the slice: x: 2, y: 2, z: 4, core: 2. Of those that a mesh axis runs over, the one named last changes fastest.
Arguments:
- mem_key: bfloat16 [128, 128, 128], P(('groups', 'mem')), parts along dimension 0, may hold values from -6 to 6
- value_base: bfloat16 [128, 128, 512], P(('groups', 'mem')), parts along dimension 0, may hold values from -6 to 6
- memory_labels: int32 [128, 128], P(('groups', 'mem')), parts along dimension 0, may hold values from 0 to 7
- valid_counts: int32 [32], P(('groups', 'mem')), parts along dimension 0, may hold values from 128 to 512, as said below
- query_key: bfloat16 [32, 64, 128], P(('groups', 'mem')), parts along dimension 0, may hold values from -96 to 96
- query_value: bfloat16 [32, 64, 512], P(('groups', 'mem')), parts along dimension 0, may hold values from -6 to 6
- object_embed: bfloat16 [8, 512], replicated, may hold values from -6 to 6
- decode_weight: bfloat16 [3, 3, 1024, 256], replicated, may hold values from -0.0625 to 0.0625
- mask_weight: bfloat16 [256, 8], replicated, may hold values from -0.375 to 0.375
Outputs:
- mask_logits: float32 [32, 64, 8], P(('groups', 'mem')), parts along dimension 0
There are 2 independent parts, one for each index of `groups`. A program takes and returns all parts, laid end to end along the dimension named above; an argument that names none is the same for every part. Nothing has to cross between parts.
Inputs may be any that keep to these rules, and one draw needn't show every extreme that they name: `valid_counts`: live positions of each memory block; some block is full and some holds a quarter.
All inputs are finite; a program needn't handle non-finite values.
Results may differ from a plain program's by a relative error of at most 0.0048.
Values may be sent and summed in bfloat16 or wider, within the bound.
No kernel may reach another device: no remote copies, remote signals or barrier semaphores. Data moves between devices by JAX's collectives and lax.ppermute only.
A program may use at most 320 MiB of HBM per device.

v0:
```python
import math
import jax
import jax.numpy as jnp
from jax import lax
from jax.sharding import PartitionSpec as P


def with_halo(block, sides, width):
    for axis, dim in sides:
        count = lax.axis_size(axis)
        forward = [(i, i + 1) for i in range(count - 1)]
        backward = [(target, source) for source, target in forward]
        low = lax.ppermute(
            lax.slice_in_dim(block, block.shape[dim] - width, None, axis=dim), axis, forward
        )
        high = lax.ppermute(lax.slice_in_dim(block, 0, width, axis=dim), axis, backward)
        block = jnp.concatenate([low, block, high], axis=dim)
    return block


def conv_taps(padded, weight, height, width):
    summed = jnp.zeros((height * width, weight.shape[3]), jnp.float32)
    for row_step in range(3):
        for col_step in range(3):
            window = padded[row_step : row_step + height, col_step : col_step + width].reshape(
                height * width, -1
            )
            summed = summed + jnp.dot(
                window, weight[row_step, col_step], preferred_element_type=jnp.float32
            )
    return summed


def shards(
    mem_key,
    value_base,
    memory_labels,
    valid_counts,
    query_key,
    query_value,
    object_embed,
    decode_weight,
    mask_weight,
):
    key_width = mem_key.shape[2]
    val_width = value_base.shape[2]
    keys_local = mem_key.reshape(-1, key_width)
    onehot = (
        memory_labels.reshape(-1)[:, None]
        == jnp.arange(object_embed.shape[0], dtype=jnp.int32)[None, :]
    ).astype(jnp.bfloat16)
    embedded = jnp.dot(onehot, object_embed, preferred_element_type=jnp.float32)
    mem_value = (value_base.reshape(-1, val_width).astype(jnp.float32) + embedded).astype(
        jnp.bfloat16
    )
    queries = lax.all_gather(query_key, "mem", axis=0, tiled=True).reshape(-1, key_width)
    block_size = keys_local.shape[0]
    scores = jnp.dot(queries, keys_local.T, preferred_element_type=jnp.float32) * (
        1.0 / math.sqrt(key_width)
    )
    is_live = (jnp.arange(block_size, dtype=jnp.int32) < valid_counts[0])[None, :]
    scores = jnp.where(is_live, scores, -jnp.inf)
    block_peak = jnp.max(scores, axis=1)
    weights = jnp.where(is_live, jnp.exp(scores - block_peak[:, None]), 0.0).astype(jnp.bfloat16)
    block_mass = jnp.sum(weights.astype(jnp.float32), axis=1)
    block_values = jnp.dot(weights, mem_value, preferred_element_type=jnp.float32)
    query_height = query_value.shape[0]
    query_width = query_value.shape[1]
    owned = query_height * query_width
    largest = lax.pmax(block_peak, "mem")
    rescale = jnp.exp(block_peak - largest)
    scaled_mass = (rescale * block_mass).reshape(-1, query_width)
    scaled_values = (rescale[:, None] * block_values).reshape(-1, query_width, val_width)
    weight_sum, value_sums = (
        lax.psum_scatter(scaled_mass, "mem", scatter_dimension=0, tiled=True),
        lax.psum_scatter(scaled_values, "mem", scatter_dimension=0, tiled=True),
    )
    weight_sum = weight_sum.reshape(owned)
    value_sums = value_sums.reshape(owned, val_width)
    readout = (
        (value_sums / weight_sum[:, None])
        .astype(jnp.bfloat16)
        .reshape(query_height, query_width, val_width)
    )
    joined = jnp.concatenate([readout, query_value], axis=-1)
    bordered = with_halo(joined, (("mem", 0),), 1)
    bordered = jnp.pad(bordered, ((0, 0), (1, 1), (0, 0)))
    hidden = jax.nn.relu(conv_taps(bordered, decode_weight, query_height, query_width)).astype(
        jnp.bfloat16
    )
    logits = jnp.dot(hidden, mask_weight, preferred_element_type=jnp.float32)
    return logits.reshape(query_height, query_width, mask_weight.shape[1])


def solution(mesh):
    placed = (
        P(("groups", "mem"), None, None),
        P(("groups", "mem"), None, None),
        P(("groups", "mem"), None),
        P(("groups", "mem")),
        P(("groups", "mem"), None, None),
        P(("groups", "mem"), None, None),
        P(),
        P(),
        P(),
    )
    return jax.shard_map(
        shards,
        mesh=mesh,
        in_specs=placed,
        out_specs=P(("groups", "mem"), None, None),
        check_vma=False,
    )
```

profile of v0, /device:TPU:5, one launch (start us, length us, event | category | flops | bytes accessed | tf_op | source)
XLA Modules:
  0.0 154.1 jit_solution(16942197713252962668)
XLA Ops:
  7.2 19.4 %all_gather.3 = bf16[16,64,128]{2,1,0:T(8,128)(2,1)S(1)} all-gather(bf16[1,64,128]{2,1,0:T(8,128)(2,1)} %param.13), channel_id=1, replica_groups=mesh['groups'=2,'mem'=16] {'mem'}, dimensions={0}, use_global_device_ids=true | all-gather | bytes 278528 | tf_op jit(solution)/shard_map/all_gather | solution.py:56
  26.6 0.5 fusion
  27.1 28.3 %pmax.7 = f32[1024]{0:T(1024)S(1)} all-reduce(f32[1024]{0:T(1024)S(1)} %get-tuple-element.9), channel_id=1, replica_groups=mesh['groups'=2,'mem'=16] {'mem'}, use_global_device_ids=true, to_apply=%region_1.2 | all-reduce | flops 1024 | bytes 8192 | tf_op jit(solution)/shard_map/pmax | solution.py:70
  55.4 0.6 convert_reduce_fusion
  56.0 3.4 %convolution_multiply_fusion = f32[1024,512]{1,0:T(8,128)} fusion(bf16[1024,512]{0,1:T(8,128)(2,1)S(1)} %get-tuple-element.8, bf16[8,512]{1,0:T(8,128)(2,1)S(1)} %copy-done.3, bf16[512,512]{1,0:T(8,128)(2,1)} %bitcast.77, f32[1024]{0:T(1024)S(1)} %get-tuple-element.6, s32[512]{0:T(512)S(1)} %bitcast.78), kind=kOutput, calls=%fused_computation.4 | convolution fusion | flops 542380032 | bytes 3684352 | tf_op jit(solution)/shard_map/dot_general | solution.py:66
  59.5 0.1 reshape.64
  59.5 0.6 dynamic-slice
  60.1 30.3 %all-reduce.1 = f32[16,64]{1,0:T(8,128)S(1)} all-reduce(f32[16,64]{1,0:T(8,128)S(1)} %reshape.64), channel_id=3, replica_groups=mesh['groups'=2,'mem'=16] {'mem'}, use_global_device_ids=true, to_apply=%region_4.5.clone | all-reduce | flops 1024 | bytes 8192
  90.5 0.7 dynamic-slice_bitcast_fusion
  91.1 30.0 %reduce-scatter.2.cloned.1.call-done = f32[1,64,512]{2,1,0:T(8,128)} async-done(((f32[16,64,512]{2,1,0:T(8,128)}), f32[1,64,512]{2,1,0:T(8,128)}) %reduce-scatter.2.cloned.1.call-update) | async-done | bytes 131088 | tf_op jit(solution)/shard_map/reduce_scatter | solution.py:76
  121.1 1.0 divide_convert_fusion
  122.1 5.8 %collective-permute-start = (bf16[1,64,1024]{2,1,0:T(8,128)(2,1)S(1)}, bf16[1,64,1024]{2,1,0:T(8,128)(2,1)S(1)}, u32[]{:S(2)}, u32[]{:S(2)}) collective-permute-start(bf16[1,64,1024]{2,1,0:T(8,128)(2,1)S(1)} %pad_maximum_fusion), channel_id=1, source_target_pairs={{0,1},{1,2},{2,3},{3,4},{4,5},{5,6},{6,7},{7,8},{8,9},{9,10},{10,1... | collective-permute-start | bytes 393224 | tf_op jit(solution)/shard_map/ppermute | solution.py:13
  127.9 1.9 %collective-permute-start.1 = (bf16[1,64,1024]{2,1,0:T(8,128)(2,1)S(1)}, bf16[1,64,1024]{2,1,0:T(8,128)(2,1)S(1)}, u32[]{:S(2)}, u32[]{:S(2)}) collective-permute-start(bf16[1,64,1024]{2,1,0:T(8,128)(2,1)S(1)} %pad_maximum_fusion), channel_id=1, source_target_pairs={{1,0},{2,1},{3,2},{4,3},{5,4},{6,5},{7,6},{8,7},{9,8},{10,9},{11,1... | collective-permute-start | bytes 393224 | tf_op jit(solution)/shard_map/ppermute | solution.py:16
  129.8 5.2 %collective-permute-done.1 = bf16[1,64,1024]{2,1,0:T(8,128)(2,1)S(1)} collective-permute-done((bf16[1,64,1024]{2,1,0:T(8,128)(2,1)S(1)}, bf16[1,64,1024]{2,1,0:T(8,128)(2,1)S(1)}, u32[]{:S(2)}, u32[]{:S(2)}) %collective-permute-start.1) | collective-permute-done | bytes 131104 | tf_op jit(solution)/shard_map/ppermute | solution.py:16
  135.1 0.1 select_maximum_fusion
  135.2 1.2 fusion.19
  136.5 1.2 fusion.9
  137.7 1.3 convolution_add_fusion.7
  139.0 1.3 convolution_add_fusion.6
  140.3 1.3 convolution_add_fusion.5
  141.5 1.3 convolution_add_fusion.4
  142.8 1.3 convolution_add_fusion.3
  144.0 1.3 convolution_add_fusion.2
  145.3 2.0 %fusion.6 = f32[1,64,8]{1,2,0:T(8,128)} fusion(bf16[256,8]{0,1:T(8,128)(2,1)S(1)} %copy-done.2, f32[64,256]{1,0:T(8,128)S(1)} %fusion.9, f32[64,256]{1,0:T(8,128)S(1)} %convolution_add_fusion.2, bf16[3,3,1024,256]{3,2,1,0:T(8,128)(2,1)} %param.16, bf16[1,64,1024]{2,1,0:T(8,128)(2,1)S(1)} %collective-permute-done.1), kind=kOutput, calls=%fused_computation.20 | convolution fusion | flops 33882112 | bytes 792576 | tf_op jit(solution)/shard_map/dot_general | solution.py:91
  (18 shorter events, 0.1 us)
Async XLA Ops:
  6.5 20.1 %copy-start = (bf16[4,128,128]{2,1,0:T(8,128)(2,1)S(1)}, bf16[4,128,128]{2,1,0:T(8,128)(2,1)}, u32[]{:S(2)}) copy-start(bf16[4,128,128]{2,1,0:T(8,128)(2,1)} %param.9) | copy-start | bytes 393220
  6.5 114.5 %reduce-scatter.2.cloned.1.call-start = ((), (), s32[]{:S(2)}) async-start(), calls=%async_computation.1 | async-start | bytes 2228224 | tf_op jit(solution)/shard_map/reduce_scatter | solution.py:76
  27.1 28.9 %copy-start.3 = (bf16[8,512]{1,0:T(8,128)(2,1)S(1)}, bf16[8,512]{1,0:T(8,128)(2,1)}, u32[]{:S(2)}) copy-start(bf16[8,512]{1,0:T(8,128)(2,1)} %param.15) | copy-start | bytes 24580
  27.1 28.9 %copy-start.4 = (s32[4,128]{1,0:T(4,128)S(1)}, s32[4,128]{1,0:T(4,128)}, u32[]{:S(2)}) copy-start(s32[4,128]{1,0:T(4,128)} %param.11) | copy-start | bytes 6148
  56.0 3.5 %copy-start.5 = (u32[32]{0:T(128)S(1)}, u32[32]{0:T(128)}, u32[]{:S(2)}) copy-start(u32[32]{0:T(128)} %constant.21) | copy-start | bytes 388
  59.4 62.6 %copy-start.1 = (bf16[1,64,512]{2,1,0:T(8,128)(2,1)S(1)}, bf16[1,64,512]{2,1,0:T(8,128)(2,1)}, u32[]{:S(2)}) copy-start(bf16[1,64,512]{2,1,0:T(8,128)(2,1)} %param.14) | copy-start | bytes 196612
  122.1 7.7 %collective-permute-start = (bf16[1,64,1024]{2,1,0:T(8,128)(2,1)S(1)}, bf16[1,64,1024]{2,1,0:T(8,128)(2,1)S(1)}, u32[]{:S(2)}, u32[]{:S(2)}) collective-permute-start(bf16[1,64,1024]{2,1,0:T(8,128)(2,1)S(1)} %pad_maximum_fusion), channel_id=1, source_target_pairs={{0,1},{1,2},{2,3},{3,4},{4,5},{5,6},{6,7},{7,8},{8,9},{9,10},{10,1... | collective-permute-start | bytes 393224 | tf_op jit(solution)/shard_map/ppermute | solution.py:13
  127.9 7.2 %collective-permute-start.1 = (bf16[1,64,1024]{2,1,0:T(8,128)(2,1)S(1)}, bf16[1,64,1024]{2,1,0:T(8,128)(2,1)S(1)}, u32[]{:S(2)}, u32[]{:S(2)}) collective-permute-start(bf16[1,64,1024]{2,1,0:T(8,128)(2,1)S(1)} %pad_maximum_fusion), channel_id=1, source_target_pairs={{1,0},{2,1},{3,2},{4,3},{5,4},{6,5},{7,6},{8,7},{9,8},{10,9},{11,1... | collective-permute-start | bytes 393224 | tf_op jit(solution)/shard_map/ppermute | solution.py:16
  139.0 6.3 %copy-start.2 = (bf16[256,8]{0,1:T(8,128)(2,1)S(1)}, bf16[256,8]{0,1:T(8,128)(2,1)}, u32[]{:S(2)}) copy-start(bf16[256,8]{0,1:T(8,128)(2,1)} %param.17) | copy-start | bytes 12292
Sparse Core Ops, SparseCore 0:
  59.6 61.4 reduce-scatter.1
where the time goes:
time: 155 us; the launch traced here: 154 us
  blocking collectives  78 us (50%)
  waiting for transfers between devices  35.2 us (23%)
  matrix products  15.8 us (10%)
  between operations  14.3 us (9%)
  starting transfers between devices  7.7 us (5%)
  other arithmetic  1.72 us (1%)
    unnamed x1, blocking collectives  30.3 us
    reduce_scatter x1, waiting for transfers between devices, shards(): lax.psum_scatter(scaled_values, 'mem', scatter_dimension=0, tiled=True)  30 us
    pmax x1, blocking collectives, shards(): largest = lax.pmax(block_peak, 'mem')  28.3 us
    all_gather x1, blocking collectives, shards(): lax.all_gather(query_key, 'mem', axis=0, tiled=True).reshape(-1, key_width)  19.4 us
    dot_general x8, matrix products, conv_taps(): jnp.dot(window, weight[row_step, col_step], preferred_element_type=jnp.fl...  10 us
    ppermute x1, starting transfers between devices, with_halo(): lax.ppermute(lax.slice_in_dim(block, block.shape[dim] - width, None, axis...  5.78 us
    ppermute x1, waiting for transfers between devices, with_halo(): lax.ppermute(lax.slice_in_dim(block, 0, width, axis=dim), axis, backward)  5.25 us
    dot_general x1, matrix products, shards(): jnp.dot(weights, mem_value, preferred_element_type=jnp.float32)  3.39 us
  transfers between devices with their start and end apart: 3, of which 2 were waited for; matrix products, arithmetic and copies ran while one was open for 1% of the time, Pallas kernels for 0%

commit v1 on v0

--- a/solution.py
+++ b/solution.py
@@ -3,6 +3,18 @@
 import jax.numpy as jnp
 from jax import lax
 from jax.sharding import PartitionSpec as P
+
+
+def gather_by_bits(array, axis, dim):
+    ways, here = (lax.axis_size(axis), lax.axis_index(axis))
+    grown, reach = (array, 1)
+    while reach < ways:
+        theirs = lax.ppermute(grown, axis, [(d, d ^ reach) for d in range(ways)])
+        mine_first = jnp.concatenate([grown, theirs], axis=dim)
+        theirs_first = jnp.concatenate([theirs, grown], axis=dim)
+        grown = jnp.where(here & reach == 0, mine_first, theirs_first)
+        reach = 2 * reach
+    return grown
 
 
 def with_halo(block, sides, width):
@@ -53,7 +65,7 @@
     mem_value = (value_base.reshape(-1, val_width).astype(jnp.float32) + embedded).astype(
         jnp.bfloat16
     )
-    queries = lax.all_gather(query_key, "mem", axis=0, tiled=True).reshape(-1, key_width)
+    queries = gather_by_bits(query_key, "mem", 0).reshape(-1, key_width)
     block_size = keys_local.shape[0]
     scores = jnp.dot(queries, keys_local.T, preferred_element_type=jnp.float32) * (
         1.0 / math.sqrt(key_width)

time: 155 us -> 150 us (0.968)
  blocking collectives: 78 us -> 58.9 us
  waiting for transfers between devices: 35.2 us -> 43.9 us
  starting transfers between devices: 7.7 us -> 12.1 us
    all_gather x1 -> x0, blocking collectives: 19.4 us -> none  [shards(): lax.all_gather(query_key, 'mem', axis=0, tiled=True).reshape(-1, key_width)]
    ppermute x0 -> x4, waiting for transfers between devices: none -> 8.77 us  [gather_by_bits(): theirs = lax.ppermute(grown, axis, [(d, d ^ reach) for d in range(ways)])]
    ppermute x0 -> x4, starting transfers between devices: none -> 4.41 us  [gather_by_bits(): theirs = lax.ppermute(grown, axis, [(d, d ^ reach) for d in range(ways)])]
  transfers between devices with their start and end apart: 3 -> 7, of which waited for: 2 -> 6; matrix products, arithmetic and copies ran while one was open for 1% -> 1% of each run, Pallas kernels for 0% -> 0%
where the time goes in v1:
time: 150 us; the launch traced here: 149 us
  blocking collectives  58.9 us (39%)
  waiting for transfers between devices  43.9 us (29%)
  matrix products  15.8 us (11%)
  between operations  14.3 us (10%)
  starting transfers between devices  12.1 us (8%)
  other arithmetic  2.57 us (2%)
    unnamed x1, blocking collectives  30.6 us
    reduce_scatter x1, waiting for transfers between devices, shards(): lax.psum_scatter(scaled_values, 'mem', scatter_dimension=0, tiled=True)  29.9 us
    pmax x1, blocking collectives, shards(): largest = lax.pmax(block_peak, 'mem')  28.3 us
    dot_general x8, matrix products, conv_taps(): jnp.dot(window, weight[row_step, col_step], preferred_element_type=jnp.fl...  10 us
    ppermute x4, waiting for transfers between devices, gather_by_bits(): theirs = lax.ppermute(grown, axis, [(d, d ^ reach) for d in range(ways)])  8.77 us
    ppermute x1, starting transfers between devices, with_halo(): lax.ppermute(lax.slice_in_dim(block, block.shape[dim] - width, None, axis...  5.75 us
    ppermute x1, waiting for transfers between devices, with_halo(): lax.ppermute(lax.slice_in_dim(block, 0, width, axis=dim), axis, backward)  5.25 us
    ppermute x4, starting transfers between devices, gather_by_bits(): theirs = lax.ppermute(grown, axis, [(d, d ^ reach) for d in range(ways)])  4.41 us
  transfers between devices with their start and end apart: 7, of which 6 were waited for; matrix products, arithmetic and copies ran while one was open for 1% of the time, Pallas kernels for 0%

profile of v1, /device:TPU:5, one launch (start us, length us, event | category | flops | bytes accessed | tf_op | source)
XLA Modules:
  0.0 149.0 jit_solution(10157949938138788741)
XLA Ops:
  7.2 1.0 collective-permute-done
  8.3 0.8 maximum_select_fusion.3
  9.1 2.8 %collective-permute-done.1 = bf16[2,64,128]{2,1,0:T(8,128)(2,1)S(1)} collective-permute-done((bf16[2,64,128]{2,1,0:T(8,128)(2,1)S(1)}, bf16[2,64,128]{2,1,0:T(8,128)(2,1)S(1)}, u32[]{:S(2)}, u32[]{:S(2)}) %collective-permute-start.1) | collective-permute-done | bytes 32800 | tf_op jit(solution)/shard_map/ppermute | solution.py:12
  11.8 1.4 collective-permute-start.2
  13.2 1.8 %collective-permute-done.2 = bf16[4,64,128]{2,1,0:T(8,128)(2,1)S(1)} collective-permute-done((bf16[4,64,128]{2,1,0:T(8,128)(2,1)S(1)}, bf16[4,64,128]{2,1,0:T(8,128)(2,1)S(1)}, u32[]{:S(2)}, u32[]{:S(2)}) %collective-permute-start.2) | collective-permute-done | bytes 65568 | tf_op jit(solution)/shard_map/ppermute | solution.py:12
  15.0 2.4 %collective-permute-start.3 = (bf16[8,64,128]{2,1,0:T(8,128)(2,1)S(1)}, bf16[8,64,128]{2,1,0:T(8,128)(2,1)S(1)}, u32[]{:S(2)}, u32[]{:S(2)}) collective-permute-start(bf16[8,64,128]{2,1,0:T(8,128)(2,1)S(1)} %maximum_select_fusion.1), channel_id=1, source_target_pairs={{0,8},{1,9},{2,10},{3,11},{4,12},{5,13},{6,14},{7,15},{8,0},{9,1},... | collective-permute-start | bytes 393224 | tf_op jit(solution)/shard_map/ppermute | solution.py:12
  18.1 3.1 %collective-permute-done.3 = bf16[8,64,128]{2,1,0:T(8,128)(2,1)S(1)} collective-permute-done((bf16[8,64,128]{2,1,0:T(8,128)(2,1)S(1)}, bf16[8,64,128]{2,1,0:T(8,128)(2,1)S(1)}, u32[]{:S(2)}, u32[]{:S(2)}) %collective-permute-start.3) | collective-permute-done | bytes 131104 | tf_op jit(solution)/shard_map/ppermute | solution.py:12
  21.8 28.3 %pmax.7 = f32[1024]{0:T(1024)S(1)} all-reduce(f32[1024]{0:T(1024)S(1)} %get-tuple-element.9), channel_id=1, replica_groups=mesh['groups'=2,'mem'=16] {'mem'}, use_global_device_ids=true, to_apply=%region_1.2 | all-reduce | flops 1024 | bytes 8192 | tf_op jit(solution)/shard_map/pmax | solution.py:82
  50.7 3.4 %convolution_multiply_fusion = f32[1024,512]{1,0:T(8,128)} fusion(bf16[1024,512]{0,1:T(8,128)(2,1)S(1)} %get-tuple-element.8, bf16[8,512]{1,0:T(8,128)(2,1)S(1)} %copy-done.3, bf16[512,512]{1,0:T(8,128)(2,1)} %bitcast.77, f32[1024]{0:T(1024)S(1)} %get-tuple-element.6, s32[512]{0:T(512)S(1)} %bitcast.78), kind=kOutput, calls=%fused_computation.4 | convolution fusion | flops 542380032 | bytes 3684352 | tf_op jit(solution)/shard_map/dot_general | solution.py:78
  54.8 30.6 %all-reduce.1 = f32[16,64]{1,0:T(8,128)S(1)} all-reduce(f32[16,64]{1,0:T(8,128)S(1)} %reshape.73), channel_id=3, replica_groups=mesh['groups'=2,'mem'=16] {'mem'}, use_global_device_ids=true, to_apply=%region_4.5.clone | all-reduce | flops 1024 | bytes 8192
  86.1 29.9 %reduce-scatter.2.cloned.1.call-done = f32[1,64,512]{2,1,0:T(8,128)} async-done(((f32[16,64,512]{2,1,0:T(8,128)}), f32[1,64,512]{2,1,0:T(8,128)}) %reduce-scatter.2.cloned.1.call-update) | async-done | bytes 131088 | tf_op jit(solution)/shard_map/reduce_scatter | solution.py:88
  116.0 1.0 divide_convert_fusion
  117.0 5.7 %collective-permute-start.4 = (bf16[1,64,1024]{2,1,0:T(8,128)(2,1)S(1)}, bf16[1,64,1024]{2,1,0:T(8,128)(2,1)S(1)}, u32[]{:S(2)}, u32[]{:S(2)}) collective-permute-start(bf16[1,64,1024]{2,1,0:T(8,128)(2,1)S(1)} %pad_maximum_fusion), channel_id=1, source_target_pairs={{0,1},{1,2},{2,3},{3,4},{4,5},{5,6},{6,7},{7,8},{8,9},{9,10},{10,1... | collective-permute-start | bytes 393224 | tf_op jit(solution)/shard_map/ppermute | solution.py:25
  122.7 1.9 %collective-permute-start.5 = (bf16[1,64,1024]{2,1,0:T(8,128)(2,1)S(1)}, bf16[1,64,1024]{2,1,0:T(8,128)(2,1)S(1)}, u32[]{:S(2)}, u32[]{:S(2)}) collective-permute-start(bf16[1,64,1024]{2,1,0:T(8,128)(2,1)S(1)} %pad_maximum_fusion), channel_id=1, source_target_pairs={{1,0},{2,1},{3,2},{4,3},{5,4},{6,5},{7,6},{8,7},{9,8},{10,9},{11,1... | collective-permute-start | bytes 393224 | tf_op jit(solution)/shard_map/ppermute | solution.py:28
  124.7 5.2 %collective-permute-done.5 = bf16[1,64,1024]{2,1,0:T(8,128)(2,1)S(1)} collective-permute-done((bf16[1,64,1024]{2,1,0:T(8,128)(2,1)S(1)}, bf16[1,64,1024]{2,1,0:T(8,128)(2,1)S(1)}, u32[]{:S(2)}, u32[]{:S(2)}) %collective-permute-start.5) | collective-permute-done | bytes 131104 | tf_op jit(solution)/shard_map/ppermute | solution.py:28
  130.0 1.2 fusion.19
  131.3 1.2 fusion.9
  132.6 1.3 convolution_add_fusion.7
  133.8 1.3 convolution_add_fusion.6
  135.1 1.3 convolution_add_fusion.5
  136.4 1.3 convolution_add_fusion.4
  137.6 1.3 convolution_add_fusion.3
  138.9 1.3 convolution_add_fusion.2
  140.1 2.0 %fusion.6 = f32[1,64,8]{1,2,0:T(8,128)} fusion(bf16[256,8]{0,1:T(8,128)(2,1)S(1)} %copy-done.2, f32[64,256]{1,0:T(8,128)S(1)} %fusion.9, f32[64,256]{1,0:T(8,128)S(1)} %convolution_add_fusion.2, bf16[3,3,1024,256]{3,2,1,0:T(8,128)(2,1)} %param.16, bf16[1,64,1024]{2,1,0:T(8,128)(2,1)S(1)} %collective-permute-done.5), kind=kOutput, calls=%fused_computation.20 | convolution fusion | flops 33882112 | bytes 792576 | tf_op jit(solution)/shard_map/dot_general | solution.py:103
  (29 shorter events, 3.3 us)
Async XLA Ops:
  6.5 14.7 %copy-start = (bf16[4,128,128]{2,1,0:T(8,128)(2,1)S(1)}, bf16[4,128,128]{2,1,0:T(8,128)(2,1)}, u32[]{:S(2)}) copy-start(bf16[4,128,128]{2,1,0:T(8,128)(2,1)} %param.9) | copy-start | bytes 393220
  6.5 109.4 %reduce-scatter.2.cloned.1.call-start = ((), (), s32[]{:S(2)}) async-start(), calls=%async_computation.1 | async-start | bytes 2228224 | tf_op jit(solution)/shard_map/reduce_scatter | solution.py:88
  6.5 1.7 %collective-permute-start = (bf16[1,64,128]{2,1,0:T(8,128)(2,1)}, bf16[1,64,128]{2,1,0:T(8,128)(2,1)S(1)}, u32[]{:S(2)}, u32[]{:S(2)}) collective-permute-start(bf16[1,64,128]{2,1,0:T(8,128)(2,1)} %param.13), channel_id=1, source_target_pairs={{0,1},{1,0},{2,3},{3,2},{4,5},{5,4},{6,7},{7,6},{8,9},{9,8},{10,11... | collective-permute-start | bytes 49160 | tf_op jit(solution)/shard_map/ppermute | solution.py:12
  9.1 2.8 %collective-permute-start.1 = (bf16[2,64,128]{2,1,0:T(8,128)(2,1)S(1)}, bf16[2,64,128]{2,1,0:T(8,128)(2,1)S(1)}, u32[]{:S(2)}, u32[]{:S(2)}) collective-permute-start(bf16[2,64,128]{2,1,0:T(8,128)(2,1)S(1)} %maximum_select_fusion.3), channel_id=1, source_target_pairs={{0,2},{1,3},{2,0},{3,1},{4,6},{5,7},{6,4},{7,5},{8,10},{9,11},{10,... | collective-permute-start | bytes 98312 | tf_op jit(solution)/shard_map/ppermute | solution.py:12
  11.8 3.2 %collective-permute-start.2 = (bf16[4,64,128]{2,1,0:T(8,128)(2,1)S(1)}, bf16[4,64,128]{2,1,0:T(8,128)(2,1)S(1)}, u32[]{:S(2)}, u32[]{:S(2)}) collective-permute-start(bf16[4,64,128]{2,1,0:T(8,128)(2,1)S(1)} %maximum_select_fusion.2), channel_id=1, source_target_pairs={{0,4},{1,5},{2,6},{3,7},{4,0},{5,1},{6,2},{7,3},{8,12},{9,13},{10,... | collective-permute-start | bytes 196616 | tf_op jit(solution)/shard_map/ppermute | solution.py:12
  15.0 6.2 %collective-permute-start.3 = (bf16[8,64,128]{2,1,0:T(8,128)(2,1)S(1)}, bf16[8,64,128]{2,1,0:T(8,128)(2,1)S(1)}, u32[]{:S(2)}, u32[]{:S(2)}) collective-permute-start(bf16[8,64,128]{2,1,0:T(8,128)(2,1)S(1)} %maximum_select_fusion.1), channel_id=1, source_target_pairs={{0,8},{1,9},{2,10},{3,11},{4,12},{5,13},{6,14},{7,15},{8,0},{9,1},... | collective-permute-start | bytes 393224 | tf_op jit(solution)/shard_map/ppermute | solution.py:12
  21.7 29.0 %copy-start.3 = (bf16[8,512]{1,0:T(8,128)(2,1)S(1)}, bf16[8,512]{1,0:T(8,128)(2,1)}, u32[]{:S(2)}) copy-start(bf16[8,512]{1,0:T(8,128)(2,1)} %param.15) | copy-start | bytes 24580
  21.7 29.0 %copy-start.4 = (s32[4,128]{1,0:T(4,128)S(1)}, s32[4,128]{1,0:T(4,128)}, u32[]{:S(2)}) copy-start(s32[4,128]{1,0:T(4,128)} %param.11) | copy-start | bytes 6148
  50.7 3.4 %copy-start.5 = (u32[32]{0:T(128)S(1)}, u32[32]{0:T(128)}, u32[]{:S(2)}) copy-start(u32[32]{0:T(128)} %constant.34) | copy-start | bytes 388
  54.1 62.9 %copy-start.1 = (bf16[1,64,512]{2,1,0:T(8,128)(2,1)S(1)}, bf16[1,64,512]{2,1,0:T(8,128)(2,1)}, u32[]{:S(2)}) copy-start(bf16[1,64,512]{2,1,0:T(8,128)(2,1)} %param.14) | copy-start | bytes 196612
  117.0 7.7 %collective-permute-start.4 = (bf16[1,64,1024]{2,1,0:T(8,128)(2,1)S(1)}, bf16[1,64,1024]{2,1,0:T(8,128)(2,1)S(1)}, u32[]{:S(2)}, u32[]{:S(2)}) collective-permute-start(bf16[1,64,1024]{2,1,0:T(8,128)(2,1)S(1)} %pad_maximum_fusion), channel_id=1, source_target_pairs={{0,1},{1,2},{2,3},{3,4},{4,5},{5,6},{6,7},{7,8},{8,9},{9,10},{10,1... | collective-permute-start | bytes 393224 | tf_op jit(solution)/shard_map/ppermute | solution.py:25
  122.7 7.2 %collective-permute-start.5 = (bf16[1,64,1024]{2,1,0:T(8,128)(2,1)S(1)}, bf16[1,64,1024]{2,1,0:T(8,128)(2,1)S(1)}, u32[]{:S(2)}, u32[]{:S(2)}) collective-permute-start(bf16[1,64,1024]{2,1,0:T(8,128)(2,1)S(1)} %pad_maximum_fusion), channel_id=1, source_target_pairs={{1,0},{2,1},{3,2},{4,3},{5,4},{6,5},{7,6},{8,7},{9,8},{10,9},{11,1... | collective-permute-start | bytes 393224 | tf_op jit(solution)/shard_map/ppermute | solution.py:28
  133.8 6.3 %copy-start.2 = (bf16[256,8]{0,1:T(8,128)(2,1)S(1)}, bf16[256,8]{0,1:T(8,128)(2,1)}, u32[]{:S(2)}) copy-start(bf16[256,8]{0,1:T(8,128)(2,1)} %param.17) | copy-start | bytes 12292
Sparse Core Ops, SparseCore 0:
  54.2 61.6 reduce-scatter.1
